TPU v7x, 256 devices: a whole 4x4x8 slice. The times are simulated.
256 devices in a mesh: gen: 8 (over y, core), bus: 32 (over x, z).
Axes of the slice: x: 4, y: 4, z: 8, core: 2. Of those that a mesh axis runs over, the one named last changes fastest.
Arguments:
- bus_price: float32 [32, 12, 16384], P(None, None, 'bus'), may hold values from -4 to 4
- bus_demand: float32 [32, 12, 16384], P('gen', None, 'bus'), may hold values from 0 to 2
- multipliers: float32 [2, 32, 12, 24576], P(None, 'gen', None, 'bus'), may hold values from 0 to 1
- line_limits: float32 [24576], P('bus'), may hold values from 0.3 to 3
- ptdf_blocks: bfloat16 [192, 16, 128, 128], P('bus'), may hold values from -0.125 to 0.125
- ptdf_pattern: int32 [192, 16], P('bus'), may hold values from 0 to 127, as said below
- gen_bus: int32 [4096], P(('gen', 'bus')), may hold values from 0 to 16383, as said below
- state_counts: int32 [4096], P(('gen', 'bus')), may hold values from 64 to 512, as said below
- transitions: int32 [4096, 3, 512], P(('gen', 'bus')), may hold values from 0 to 511, as said below
- state_level: float32 [4096, 512], P(('gen', 'bus')), may hold values from 0 to 3
- state_cost: float32 [4096, 512], P(('gen', 'bus')), may hold values from 0 to 2
Outputs:
- new_multipliers: float32 [2, 32, 12, 24576], P(None, 'gen', None, 'bus')
- new_price: float32 [32, 12, 16384], P(None, None, 'bus')
Inputs may be any that keep to these rules, and one draw needn't show every extreme that they name: Generator i sits in bus block (i // 16) % 32: gen_bus[i] // 512 equals that number. `state_counts`: among the generators of each aligned group of 16, at most 6 have a count above 256, and some group has exactly 6. `transitions`: every successor of a state below its generator's count is below that count; a state at or above the count has itself as every successor. `ptdf_pattern`: the 16 bus blocks named in one row are different.
All inputs are finite; a program needn't handle non-finite values.
Results may differ from a plain program's by a relative error of at most 0.0031.
Values may be sent and summed in bfloat16 or wider, within the bound.
A program may use at most 128 MiB of HBM per device.

v0:
```python
import jax
import jax.numpy as jnp
from jax import lax
from jax.sharding import PartitionSpec as P

STATES = 512
BLK = 128
NNZB = 16
HIGHEST_PRECISION = lax.Precision.HIGHEST
STEP_SIZE = 1.0


def successor_matrix(trans_rows, state_span):
    columns = jnp.arange(state_span, dtype=jnp.int32)
    operator_table = jnp.zeros((trans_rows.shape[0], state_span, state_span), jnp.bfloat16)
    for branch in range(trans_rows.shape[1]):
        operator_table = operator_table + (
            trans_rows[:, branch, :state_span, None] == columns[None, None, :]
        ).astype(jnp.bfloat16)
    return operator_table


def smoothed_plan(level_rows, cost_rows, valid_rows, operator_table, hourly_prices):
    weights = valid_rows[None, :, None, :] * jnp.exp(
        hourly_prices[..., None] * level_rows[None, :, None, :] - cost_rows[None, :, None, :]
    )
    opening = weights[0] / jnp.sum(weights[0], axis=-1, keepdims=True)

    def forward(state_now, present_weight):
        pushed = jnp.einsum(
            "hkj,hjf->hkf",
            state_now.astype(jnp.bfloat16),
            operator_table,
            preferred_element_type=jnp.float32,
        )
        raised = pushed * present_weight
        scale_now = jnp.sum(raised, axis=-1, keepdims=True)
        state_next = raised / scale_now
        return (state_next, (state_next, scale_now))

    unused_state, (states_later, scales) = lax.scan(forward, opening, weights[1:])
    states_all = jnp.concatenate([opening[None], states_later], axis=0)

    def backward(back_now, inputs):
        present_weight, scale_now = inputs
        fetched_entries = (present_weight * back_now / scale_now).astype(jnp.bfloat16)
        back_prev = jnp.einsum(
            "fjc,fhc->fjh", fetched_entries, operator_table, preferred_element_type=jnp.float32
        )
        return (back_prev, back_prev)

    ones_back = jnp.ones_like(opening)
    unused_back, backs_earlier = lax.scan(backward, ones_back, (weights[1:], scales), reverse=True)
    backs_all = jnp.concatenate([backs_earlier, ones_back[None]], axis=0)
    combined_probability = states_all * backs_all
    return jnp.sum(combined_probability * level_rows[None, :, None, :], axis=-1) / jnp.sum(
        combined_probability, axis=-1
    )


def shards(
    bus_price,
    bus_demand,
    multipliers,
    line_limits,
    ptdf_blocks,
    ptdf_pattern,
    gen_bus,
    state_counts,
    transitions,
    state_level,
    state_cost,
):
    scn_all, hour_count, bus_dev = bus_price.shape
    scn_dev = bus_demand.shape[0]
    gen_index = lax.axis_index("gen")
    bus_index = lax.axis_index("bus")
    block_total = lax.axis_size("bus") * bus_dev // BLK
    local_bus = gen_bus - bus_index * bus_dev
    onehot_all = (local_bus[:, None] == jnp.arange(bus_dev, dtype=jnp.int32)[None, :]).astype(
        jnp.float32
    )
    valid_all = (jnp.arange(STATES, dtype=jnp.int32)[None, :] < state_counts[:, None]).astype(
        jnp.float32
    )
    operator_table = successor_matrix(transitions, STATES)
    hourly_prices = jnp.einsum("rtb,gb->tgr", bus_price, onehot_all, precision=HIGHEST_PRECISION)
    output = smoothed_plan(state_level, state_cost, valid_all, operator_table, hourly_prices)
    summed = jnp.einsum("tgr,gb->rtb", output, onehot_all, precision=HIGHEST_PRECISION)
    injections = lax.psum_scatter(summed, "gen", scatter_dimension=0, tiled=True)
    row_total = scn_dev * hour_count
    network_row_block = (injections - bus_demand).astype(jnp.bfloat16).reshape(row_total, bus_dev)
    line_blocks = ptdf_blocks.shape[0]
    wanted = ptdf_pattern.reshape(-1)
    piece_cols = lax.all_gather(network_row_block, "bus", axis=1, tiled=True)
    block_count = piece_cols.shape[1] // BLK
    block_ids = jnp.arange(block_count, dtype=jnp.int32)
    chooser = (wanted[:, None] == block_ids[None, :]).astype(jnp.bfloat16)
    blocked = piece_cols.reshape(piece_cols.shape[0], block_count, BLK)
    picked_blocks = jnp.einsum("rjb,mj->rmb", blocked, chooser, preferred_element_type=jnp.float32)
    gathered = picked_blocks.astype(jnp.bfloat16).reshape(row_total, line_blocks, NNZB, BLK)
    flows = jnp.einsum("rlkb,lkbc->rlc", gathered, ptdf_blocks, preferred_element_type=jnp.float32)
    flow_lines = flows.reshape(scn_dev, hour_count, line_blocks * BLK)
    upper_old = multipliers[0]
    lower_old = multipliers[1]
    upper_new = jnp.maximum(0.0, upper_old + STEP_SIZE * (flow_lines - line_limits[None, None, :]))
    lower_new = jnp.maximum(0.0, lower_old + STEP_SIZE * (-flow_lines - line_limits[None, None, :]))
    change = (
        (upper_new - upper_old - (lower_new - lower_old))
        .astype(jnp.bfloat16)
        .reshape(row_total, line_blocks, BLK)
    )
    spread = jnp.einsum("rlc,lkbc->rlkb", change, ptdf_blocks, preferred_element_type=jnp.float32)
    placing = (
        ptdf_pattern[:, :, None] == jnp.arange(block_total, dtype=jnp.int32)[None, None, :]
    ).astype(jnp.float32)
    partial_change = jnp.einsum(
        "rlkb,lkj->rjb", spread, placing, precision=HIGHEST_PRECISION
    ).reshape(scn_dev, hour_count, block_total * BLK)
    own_change = lax.psum_scatter(partial_change, "bus", scatter_dimension=2, tiled=True)
    own_price = lax.dynamic_slice_in_dim(bus_price, gen_index * scn_dev, scn_dev, 0)
    new_share = own_price - own_change
    new_price = lax.all_gather(new_share, "gen", axis=0, tiled=True)
    return (jnp.stack([upper_new, lower_new]), new_price)


def solution(mesh):
    in_specs = (
        P(None, None, "bus"),
        P("gen", None, "bus"),
        P(None, "gen", None, "bus"),
        P("bus"),
        P("bus", None, None, None),
        P("bus", None),
        P(("gen", "bus")),
        P(("gen", "bus")),
        P(("gen", "bus"), None, None),
        P(("gen", "bus"), None),
        P(("gen", "bus"), None),
    )
    out_specs = (P(None, "gen", None, "bus"), P(None, None, "bus"))
    return jax.shard_map(shards, mesh=mesh, in_specs=in_specs, out_specs=out_specs, check_vma=False)
```

profile of v0, /device:TPU:1, one launch (start us, length us, event | category | flops | bytes accessed | tf_op | source)
XLA Modules:
  0.0 687.4 jit_solution(12709552428947251052)
XLA Ops:
  8.8 2.0 convolution_bitcast_fusion.2
  10.8 3.3 exponential_multiply_fusion
  15.4 3.4 copy-done.1
  19.9 11.2 %slice.31 = f32[11,16,32,512]{3,2,1,0:T(8,128)} slice(f32[12,16,32,512]{3,2,1,0:T(8,128)} %copy-done.1), slice={[1:12], [0:16], [0:32], [0:512]} | slice | bytes 23068672 | tf_op jit(solution)/shard_map/slice | solution.py:41
  31.1 5.7 broadcast.49.clone
  36.8 103.0 %while.32 = (s32[]{:T(128)}, bf16[16,32,512]{2,1,0:T(8,128)(2,1)}, f32[11,16,32,512]{3,2,1,0:T(8,128)}, f32[11,16,32,1]{2,1,3,0:T(8,128)S(1)}, f32[11,16,32,512]...) while((s32[]{:T(128)}, bf16[16,32,512]{2,1,0:T(8,128)(2,1)}, ...), condition=%wide.region_3.4_spmd.clone, body=%wide.region_1.3_spmd.clone.sunk | while | flops 319815168 | bytes 5361777 | solution.py:41
  36.8 8.0 %fusion.75 = (f32[16,32]{1,0:T(8,128)S(1)}, f32[16,32,512]{2,1,0:T(8,128)S(1)}) fusion(f32[11,16,32,512]{3,2,1,0:T(8,128)} %get-tuple-element.389, s32[]{:T(128)S(6)} %copy.77, s32[16,512]{1,0:T(8,128)S(1)} %get-tuple-element.392, s32[16,512]{1,0:T(8,128)S(1)} %get-tuple-element.391, s32[16,512]{1,0:T(8,128)S(1)} %get-tuple-element.390, ...), kind=kOutput, calls=%fused_computation.83.clone.1 | convolution fusion | flops 319290880 | bytes 2721796 | tf_op jit(solution)/shard_map/while/body/eval_jaxpr/hkj,hjf->hkf/dot_general | solution.py:30
  44.8 1.3 bitcast_dynamic-update-slice_fusion.6
  46.2 8.0 %fusion.75 = (f32[16,32]{1,0:T(8,128)S(1)}, f32[16,32,512]{2,1,0:T(8,128)S(1)}) fusion(f32[11,16,32,512]{3,2,1,0:T(8,128)} %get-tuple-element.389, s32[]{:T(128)S(6)} %copy.77, s32[16,512]{1,0:T(8,128)S(1)} %get-tuple-element.392, s32[16,512]{1,0:T(8,128)S(1)} %get-tuple-element.391, s32[16,512]{1,0:T(8,128)S(1)} %get-tuple-element.390, ...), kind=kOutput, calls=%fused_computation.83.clone.1 | convolution fusion | flops 319290880 | bytes 2721796 | tf_op jit(solution)/shard_map/while/body/eval_jaxpr/hkj,hjf->hkf/dot_general | solution.py:30
  54.2 1.3 bitcast_dynamic-update-slice_fusion.6
  55.5 8.0 %fusion.75 = (f32[16,32]{1,0:T(8,128)S(1)}, f32[16,32,512]{2,1,0:T(8,128)S(1)}) fusion(f32[11,16,32,512]{3,2,1,0:T(8,128)} %get-tuple-element.389, s32[]{:T(128)S(6)} %copy.77, s32[16,512]{1,0:T(8,128)S(1)} %get-tuple-element.392, s32[16,512]{1,0:T(8,128)S(1)} %get-tuple-element.391, s32[16,512]{1,0:T(8,128)S(1)} %get-tuple-element.390, ...), kind=kOutput, calls=%fused_computation.83.clone.1 | convolution fusion | flops 319290880 | bytes 2721796 | tf_op jit(solution)/shard_map/while/body/eval_jaxpr/hkj,hjf->hkf/dot_general | solution.py:30
  63.6 1.3 bitcast_dynamic-update-slice_fusion.6
  64.9 8.0 %fusion.75 = (f32[16,32]{1,0:T(8,128)S(1)}, f32[16,32,512]{2,1,0:T(8,128)S(1)}) fusion(f32[11,16,32,512]{3,2,1,0:T(8,128)} %get-tuple-element.389, s32[]{:T(128)S(6)} %copy.77, s32[16,512]{1,0:T(8,128)S(1)} %get-tuple-element.392, s32[16,512]{1,0:T(8,128)S(1)} %get-tuple-element.391, s32[16,512]{1,0:T(8,128)S(1)} %get-tuple-element.390, ...), kind=kOutput, calls=%fused_computation.83.clone.1 | convolution fusion | flops 319290880 | bytes 2721796 | tf_op jit(solution)/shard_map/while/body/eval_jaxpr/hkj,hjf->hkf/dot_general | solution.py:30
  72.9 1.3 bitcast_dynamic-update-slice_fusion.6
  74.3 8.0 %fusion.75 = (f32[16,32]{1,0:T(8,128)S(1)}, f32[16,32,512]{2,1,0:T(8,128)S(1)}) fusion(f32[11,16,32,512]{3,2,1,0:T(8,128)} %get-tuple-element.389, s32[]{:T(128)S(6)} %copy.77, s32[16,512]{1,0:T(8,128)S(1)} %get-tuple-element.392, s32[16,512]{1,0:T(8,128)S(1)} %get-tuple-element.391, s32[16,512]{1,0:T(8,128)S(1)} %get-tuple-element.390, ...), kind=kOutput, calls=%fused_computation.83.clone.1 | convolution fusion | flops 319290880 | bytes 2721796 | tf_op jit(solution)/shard_map/while/body/eval_jaxpr/hkj,hjf->hkf/dot_general | solution.py:30
  82.3 1.3 bitcast_dynamic-update-slice_fusion.6
  83.6 8.0 %fusion.75 = (f32[16,32]{1,0:T(8,128)S(1)}, f32[16,32,512]{2,1,0:T(8,128)S(1)}) fusion(f32[11,16,32,512]{3,2,1,0:T(8,128)} %get-tuple-element.389, s32[]{:T(128)S(6)} %copy.77, s32[16,512]{1,0:T(8,128)S(1)} %get-tuple-element.392, s32[16,512]{1,0:T(8,128)S(1)} %get-tuple-element.391, s32[16,512]{1,0:T(8,128)S(1)} %get-tuple-element.390, ...), kind=kOutput, calls=%fused_computation.83.clone.1 | convolution fusion | flops 319290880 | bytes 2721796 | tf_op jit(solution)/shard_map/while/body/eval_jaxpr/hkj,hjf->hkf/dot_general | solution.py:30
  91.7 1.3 bitcast_dynamic-update-slice_fusion.6
  93.0 8.0 %fusion.75 = (f32[16,32]{1,0:T(8,128)S(1)}, f32[16,32,512]{2,1,0:T(8,128)S(1)}) fusion(f32[11,16,32,512]{3,2,1,0:T(8,128)} %get-tuple-element.389, s32[]{:T(128)S(6)} %copy.77, s32[16,512]{1,0:T(8,128)S(1)} %get-tuple-element.392, s32[16,512]{1,0:T(8,128)S(1)} %get-tuple-element.391, s32[16,512]{1,0:T(8,128)S(1)} %get-tuple-element.390, ...), kind=kOutput, calls=%fused_computation.83.clone.1 | convolution fusion | flops 319290880 | bytes 2721796 | tf_op jit(solution)/shard_map/while/body/eval_jaxpr/hkj,hjf->hkf/dot_general | solution.py:30
  101.0 1.3 bitcast_dynamic-update-slice_fusion.6
  102.4 8.0 %fusion.75 = (f32[16,32]{1,0:T(8,128)S(1)}, f32[16,32,512]{2,1,0:T(8,128)S(1)}) fusion(f32[11,16,32,512]{3,2,1,0:T(8,128)} %get-tuple-element.389, s32[]{:T(128)S(6)} %copy.77, s32[16,512]{1,0:T(8,128)S(1)} %get-tuple-element.392, s32[16,512]{1,0:T(8,128)S(1)} %get-tuple-element.391, s32[16,512]{1,0:T(8,128)S(1)} %get-tuple-element.390, ...), kind=kOutput, calls=%fused_computation.83.clone.1 | convolution fusion | flops 319290880 | bytes 2721796 | tf_op jit(solution)/shard_map/while/body/eval_jaxpr/hkj,hjf->hkf/dot_general | solution.py:30
  110.4 1.3 bitcast_dynamic-update-slice_fusion.6
  111.7 8.0 %fusion.75 = (f32[16,32]{1,0:T(8,128)S(1)}, f32[16,32,512]{2,1,0:T(8,128)S(1)}) fusion(f32[11,16,32,512]{3,2,1,0:T(8,128)} %get-tuple-element.389, s32[]{:T(128)S(6)} %copy.77, s32[16,512]{1,0:T(8,128)S(1)} %get-tuple-element.392, s32[16,512]{1,0:T(8,128)S(1)} %get-tuple-element.391, s32[16,512]{1,0:T(8,128)S(1)} %get-tuple-element.390, ...), kind=kOutput, calls=%fused_computation.83.clone.1 | convolution fusion | flops 319290880 | bytes 2721796 | tf_op jit(solution)/shard_map/while/body/eval_jaxpr/hkj,hjf->hkf/dot_general | solution.py:30
  119.8 1.3 bitcast_dynamic-update-slice_fusion.6
  121.1 8.0 %fusion.75 = (f32[16,32]{1,0:T(8,128)S(1)}, f32[16,32,512]{2,1,0:T(8,128)S(1)}) fusion(f32[11,16,32,512]{3,2,1,0:T(8,128)} %get-tuple-element.389, s32[]{:T(128)S(6)} %copy.77, s32[16,512]{1,0:T(8,128)S(1)} %get-tuple-element.392, s32[16,512]{1,0:T(8,128)S(1)} %get-tuple-element.391, s32[16,512]{1,0:T(8,128)S(1)} %get-tuple-element.390, ...), kind=kOutput, calls=%fused_computation.83.clone.1 | convolution fusion | flops 319290880 | bytes 2721796 | tf_op jit(solution)/shard_map/while/body/eval_jaxpr/hkj,hjf->hkf/dot_general | solution.py:30
  129.1 1.3 bitcast_dynamic-update-slice_fusion.6
  130.4 8.0 %fusion.75 = (f32[16,32]{1,0:T(8,128)S(1)}, f32[16,32,512]{2,1,0:T(8,128)S(1)}) fusion(f32[11,16,32,512]{3,2,1,0:T(8,128)} %get-tuple-element.389, s32[]{:T(128)S(6)} %copy.77, s32[16,512]{1,0:T(8,128)S(1)} %get-tuple-element.392, s32[16,512]{1,0:T(8,128)S(1)} %get-tuple-element.391, s32[16,512]{1,0:T(8,128)S(1)} %get-tuple-element.390, ...), kind=kOutput, calls=%fused_computation.83.clone.1 | convolution fusion | flops 319290880 | bytes 2721796 | tf_op jit(solution)/shard_map/while/body/eval_jaxpr/hkj,hjf->hkf/dot_general | solution.py:30
  138.5 1.3 bitcast_dynamic-update-slice_fusion.6
  140.9 5.8 broadcast.49
  146.8 118.3 %while.33 = (s32[]{:T(128)}, f32[16,32,512]{2,1,0:T(8,128)}, f32[11,16,32,512]{3,2,1,0:T(8,128)}, f32[11,16,32,512]{3,2,1,0:T(8,128)}, f32[11,16,32,1]{2,1,3,0:T...) while((s32[]{:T(128)}, f32[16,32,512]{2,1,0:T(8,128)}, ...), condition=%wide.region_5.6_spmd.clone, body=%wide.region_4.5_spmd.clone.sunk | while | flops 319553536 | bytes 6397045 | solution.py:53
  146.8 1.2 copy.96
  148.0 9.5 %bitcast_dynamic-update-slice_fusion.8 = (f32[11,16,32,512]{3,2,1,0:T(8,128)}, f32[16,32,512]{2,1,0:T(8,128)}) fusion(f32[11,16,32,512]{3,2,1,0:T(8,128)} %get-tuple-element.406, s32[]{:T(128)S(6)} %sub.131, s32[16,512]{1,0:T(8,128)S(1)} %get-tuple-element.421, s32[16,512]{1,0:T(8,128)S(1)} %get-tuple-element.420, ...), kind=kOutput, calls=%fused_computation.31.clone.1 | convolution fusion | flops 319553536 | bytes 4295680 | tf_op jit(solution)/shard_map/while/body/eval_jaxpr/fjc,fhc->fjh/dot_general | solution.py:47
  157.5 1.2 copy.96
  158.8 9.5 %bitcast_dynamic-update-slice_fusion.8 = (f32[11,16,32,512]{3,2,1,0:T(8,128)}, f32[16,32,512]{2,1,0:T(8,128)}) fusion(f32[11,16,32,512]{3,2,1,0:T(8,128)} %get-tuple-element.406, s32[]{:T(128)S(6)} %sub.131, s32[16,512]{1,0:T(8,128)S(1)} %get-tuple-element.421, s32[16,512]{1,0:T(8,128)S(1)} %get-tuple-element.420, ...), kind=kOutput, calls=%fused_computation.31.clone.1 | convolution fusion | flops 319553536 | bytes 4295680 | tf_op jit(solution)/shard_map/while/body/eval_jaxpr/fjc,fhc->fjh/dot_general | solution.py:47
  168.3 1.2 copy.96
  169.5 9.5 %bitcast_dynamic-update-slice_fusion.8 = (f32[11,16,32,512]{3,2,1,0:T(8,128)}, f32[16,32,512]{2,1,0:T(8,128)}) fusion(f32[11,16,32,512]{3,2,1,0:T(8,128)} %get-tuple-element.406, s32[]{:T(128)S(6)} %sub.131, s32[16,512]{1,0:T(8,128)S(1)} %get-tuple-element.421, s32[16,512]{1,0:T(8,128)S(1)} %get-tuple-element.420, ...), kind=kOutput, calls=%fused_computation.31.clone.1 | convolution fusion | flops 319553536 | bytes 4295680 | tf_op jit(solution)/shard_map/while/body/eval_jaxpr/fjc,fhc->fjh/dot_general | solution.py:47
  179.0 1.2 copy.96
  180.3 9.5 %bitcast_dynamic-update-slice_fusion.8 = (f32[11,16,32,512]{3,2,1,0:T(8,128)}, f32[16,32,512]{2,1,0:T(8,128)}) fusion(f32[11,16,32,512]{3,2,1,0:T(8,128)} %get-tuple-element.406, s32[]{:T(128)S(6)} %sub.131, s32[16,512]{1,0:T(8,128)S(1)} %get-tuple-element.421, s32[16,512]{1,0:T(8,128)S(1)} %get-tuple-element.420, ...), kind=kOutput, calls=%fused_computation.31.clone.1 | convolution fusion | flops 319553536 | bytes 4295680 | tf_op jit(solution)/shard_map/while/body/eval_jaxpr/fjc,fhc->fjh/dot_general | solution.py:47
  189.8 1.2 copy.96
  191.0 9.5 %bitcast_dynamic-update-slice_fusion.8 = (f32[11,16,32,512]{3,2,1,0:T(8,128)}, f32[16,32,512]{2,1,0:T(8,128)}) fusion(f32[11,16,32,512]{3,2,1,0:T(8,128)} %get-tuple-element.406, s32[]{:T(128)S(6)} %sub.131, s32[16,512]{1,0:T(8,128)S(1)} %get-tuple-element.421, s32[16,512]{1,0:T(8,128)S(1)} %get-tuple-element.420, ...), kind=kOutput, calls=%fused_computation.31.clone.1 | convolution fusion | flops 319553536 | bytes 4295680 | tf_op jit(solution)/shard_map/while/body/eval_jaxpr/fjc,fhc->fjh/dot_general | solution.py:47
  200.6 1.2 copy.96
  201.8 9.5 %bitcast_dynamic-update-slice_fusion.8 = (f32[11,16,32,512]{3,2,1,0:T(8,128)}, f32[16,32,512]{2,1,0:T(8,128)}) fusion(f32[11,16,32,512]{3,2,1,0:T(8,128)} %get-tuple-element.406, s32[]{:T(128)S(6)} %sub.131, s32[16,512]{1,0:T(8,128)S(1)} %get-tuple-element.421, s32[16,512]{1,0:T(8,128)S(1)} %get-tuple-element.420, ...), kind=kOutput, calls=%fused_computation.31.clone.1 | convolution fusion | flops 319553536 | bytes 4295680 | tf_op jit(solution)/shard_map/while/body/eval_jaxpr/fjc,fhc->fjh/dot_general | solution.py:47
  211.3 1.2 copy.96
  212.5 9.5 %bitcast_dynamic-update-slice_fusion.8 = (f32[11,16,32,512]{3,2,1,0:T(8,128)}, f32[16,32,512]{2,1,0:T(8,128)}) fusion(f32[11,16,32,512]{3,2,1,0:T(8,128)} %get-tuple-element.406, s32[]{:T(128)S(6)} %sub.131, s32[16,512]{1,0:T(8,128)S(1)} %get-tuple-element.421, s32[16,512]{1,0:T(8,128)S(1)} %get-tuple-element.420, ...), kind=kOutput, calls=%fused_computation.31.clone.1 | convolution fusion | flops 319553536 | bytes 4295680 | tf_op jit(solution)/shard_map/while/body/eval_jaxpr/fjc,fhc->fjh/dot_general | solution.py:47
  222.0 1.2 copy.96
  223.3 9.5 %bitcast_dynamic-update-slice_fusion.8 = (f32[11,16,32,512]{3,2,1,0:T(8,128)}, f32[16,32,512]{2,1,0:T(8,128)}) fusion(f32[11,16,32,512]{3,2,1,0:T(8,128)} %get-tuple-element.406, s32[]{:T(128)S(6)} %sub.131, s32[16,512]{1,0:T(8,128)S(1)} %get-tuple-element.421, s32[16,512]{1,0:T(8,128)S(1)} %get-tuple-element.420, ...), kind=kOutput, calls=%fused_computation.31.clone.1 | convolution fusion | flops 319553536 | bytes 4295680 | tf_op jit(solution)/shard_map/while/body/eval_jaxpr/fjc,fhc->fjh/dot_general | solution.py:47
  232.8 1.2 copy.96
  234.0 9.5 %bitcast_dynamic-update-slice_fusion.8 = (f32[11,16,32,512]{3,2,1,0:T(8,128)}, f32[16,32,512]{2,1,0:T(8,128)}) fusion(f32[11,16,32,512]{3,2,1,0:T(8,128)} %get-tuple-element.406, s32[]{:T(128)S(6)} %sub.131, s32[16,512]{1,0:T(8,128)S(1)} %get-tuple-element.421, s32[16,512]{1,0:T(8,128)S(1)} %get-tuple-element.420, ...), kind=kOutput, calls=%fused_computation.31.clone.1 | convolution fusion | flops 319553536 | bytes 4295680 | tf_op jit(solution)/shard_map/while/body/eval_jaxpr/fjc,fhc->fjh/dot_general | solution.py:47
  244.8 9.5 %bitcast_dynamic-update-slice_fusion.8 = (f32[11,16,32,512]{3,2,1,0:T(8,128)}, f32[16,32,512]{2,1,0:T(8,128)}) fusion(f32[11,16,32,512]{3,2,1,0:T(8,128)} %get-tuple-element.406, s32[]{:T(128)S(6)} %sub.131, s32[16,512]{1,0:T(8,128)S(1)} %get-tuple-element.421, s32[16,512]{1,0:T(8,128)S(1)} %get-tuple-element.420, ...), kind=kOutput, calls=%fused_computation.31.clone.1 | convolution fusion | flops 319553536 | bytes 4295680 | tf_op jit(solution)/shard_map/while/body/eval_jaxpr/fjc,fhc->fjh/dot_general | solution.py:47
  255.5 9.5 %bitcast_dynamic-update-slice_fusion.8 = (f32[11,16,32,512]{3,2,1,0:T(8,128)}, f32[16,32,512]{2,1,0:T(8,128)}) fusion(f32[11,16,32,512]{3,2,1,0:T(8,128)} %get-tuple-element.406, s32[]{:T(128)S(6)} %sub.131, s32[16,512]{1,0:T(8,128)S(1)} %get-tuple-element.421, s32[16,512]{1,0:T(8,128)S(1)} %get-tuple-element.420, ...), kind=kOutput, calls=%fused_computation.31.clone.1 | convolution fusion | flops 319553536 | bytes 4295680 | tf_op jit(solution)/shard_map/while/body/eval_jaxpr/fjc,fhc->fjh/dot_general | solution.py:47
  265.1 8.9 %fusion.37 = (f32[12,16,32]{2,1,0:T(8,128)S(1)}, f32[12,16,32]{2,1,0:T(8,128)S(1)}) fusion(f32[11,16,32,512]{3,2,1,0:T(8,128)} %get-tuple-element.159, f32[11,16,32,512]{3,2,1,0:T(8,128)} %get-tuple-element.157, f32[1,16,32,512]{3,2,1,0:T(8,128)} %slice_divide_fusion, f32[16,512]{1,0:T(8,128)S(1)} %copy-done.4), kind=kLoop, calls=%fused_computation.41 | loop fusion | flops 15716352 | bytes 24199168 | tf_op jit(solution)/shard_map/reduce_sum | solution.py:56
  273.9 1.4 convolution_bitcast_fusion.1
  276.7 67.6 %all-reduce.4.cloned.1.call-done = f32[32,12,512]{2,0,1:T(8,128)} async-done(((f32[32,12,512]{2,0,1:T(8,128)}), f32[32,12,512]{2,0,1:T(8,128)}) %all-reduce.4.cloned.1.call-update) | async-done | bytes 786448
  347.0 70.2 %all-gather.2.cloned.1.call-done = bf16[48,16384]{1,0:T(8,128)(2,1)} async-done(((bf16[48,512]{1,0:T(8,128)(2,1)}), bf16[48,16384]{1,0:T(8,128)(2,1)}) %all-gather.2.cloned.1.call-update) | async-done | bytes 1572880 | tf_op jit(solution)/shard_map/all_gather | solution.py:95
  417.2 1.8 copy.48
  422.0 1.9 add_maximum_fusion.1
  423.9 1.6 squeeze.27
  425.5 1.6 squeeze.26
  427.2 2.3 convolution_bitcast_fusion
  429.4 4.0 fusion.40
  433.4 3.7 reshape.84
  439.9 219.5 %reduce-scatter.3.cloned.1.call-done = f32[4,12,512]{2,1,0:T(8,128)} async-done(((f32[4,12,16384]{2,1,0:T(8,128)}), f32[4,12,512]{2,1,0:T(8,128)}) %reduce-scatter.3.cloned.1.call-update) | async-done | bytes 98320 | tf_op jit(solution)/shard_map/reduce_scatter | solution.py:120
  660.3 19.2 %all_gather.7 = f32[32,12,512]{2,1,0:T(8,128)S(1)} all-gather(f32[4,12,512]{2,1,0:T(8,128)S(1)} %copy_subtract_fusion), channel_id=1, replica_groups=mesh['gen'=8,'bus'=32] {'gen'}, dimensions={0}, use_global_device_ids=true | all-gather | bytes 884736 | tf_op jit(solution)/shard_map/all_gather | solution.py:123
  679.5 1.3 copy.39
  (69 shorter events, 17.8 us)
Async XLA Ops:
  7.2 412.3 %copy-start = (bf16[6,16,128,128]{3,2,1,0:T(8,128)(2,1)S(1)}, bf16[6,16,128,128]{3,2,1,0:T(8,128)(2,1)}, u32[]{:S(2)}) copy-start(bf16[6,16,128,128]{3,2,1,0:T(8,128)(2,1)} %param.19) | copy-start | bytes 9437188
  7.2 337.1 %all-reduce.4.cloned.1.call-start = ((), (), s32[]{:S(2)}) async-start(), calls=%async_computation.3 | async-start | bytes 1572864
  14.2 4.7 copy-start.1
  19.9 11.2 %copy-start.5 = (s32[16,3,512]{2,0,1:T(8,128)S(1)}, s32[16,3,512]{2,0,1:T(8,128)}, u32[]{:S(2)}) copy-start(s32[16,3,512]{2,0,1:T(8,128)} %param.23) | copy-start | bytes 294916
  146.8 118.3 %copy-start.4 = (f32[16,512]{1,0:T(8,128)S(1)}, f32[16,512]{1,0:T(8,128)}, u32[]{:S(2)}) copy-start(f32[16,512]{1,0:T(8,128)} %param.24) | copy-start | bytes 98308
  265.0 10.4 %copy-start.8 = (u32[256]{0:T(256)S(1)}, u32[256]{0:T(256)}, u32[]{:S(2)}) copy-start(u32[256]{0:T(256)} %constant.88) | copy-start | bytes 3076
  265.0 81.2 %copy-start.7 = (s32[6,16]{1,0:T(8,128)S(1)}, s32[6,16]{1,0:T(8,128)}, u32[]{:S(2)}) copy-start(s32[6,16]{1,0:T(8,128)} %param.20) | copy-start | bytes 1156
  265.0 81.2 %copy-start.3 = (f32[2,4,12,768]{3,1,2,0:T(4,128)S(1)}, f32[2,4,12,768]{3,1,2,0:T(4,128)}, u32[]{:S(2)}) copy-start(f32[2,4,12,768]{3,1,2,0:T(4,128)} %param.17) | copy-start | bytes 884740
  273.9 148.1 %copy-start.6 = (f32[768]{0:T(1024)S(1)}, f32[768]{0:T(1024)}, u32[]{:S(2)}) copy-start(f32[768]{0:T(1024)} %param.18) | copy-start | bytes 9220
  275.4 141.8 %all-gather.2.cloned.1.call-start = ((), (), s32[]{:S(2)}) async-start(), calls=%async_computation.1 | async-start | bytes 1622016 | tf_op jit(solution)/shard_map/all_gather | solution.py:95
  346.0 313.4 %reduce-scatter.3.cloned.1.call-start = ((), (), s32[]{:S(2)}) async-start(), calls=%async_computation.2 | async-start | bytes 4325376 | tf_op jit(solution)/shard_map/reduce_scatter | solution.py:120
  427.2 10.9 %copy-start.2 = (f32[1,4,12,768]{3,2,1,0:T(8,128)S(1)}, f32[1,4,12,768]{3,2,1,0:T(8,128)}, u32[]{:S(2)}) copy-start(f32[1,4,12,768]{3,2,1,0:T(8,128)} %get-tuple-element.248) | copy-start | bytes 442372
Sparse Core Ops, SparseCore 0:
  275.5 68.7 all-reduce.3
  347.3 69.8 all-gather.1
  437.2 222.1 reduce-scatter.2
where the time goes:
time: 692 us; the launch traced here: 687 us
  waiting for transfers between devices  357 us (52%)
  matrix products  204 us (29%)
  local copies, waits for them, and re-layouts  56.4 us (8%)
  other arithmetic  35.5 us (5%)
  blocking collectives  19.2 us (3%)
  between operations  14.6 us (2%)
    reduce_scatter x1, waiting for transfers between devices, shards(): lax.psum_scatter(partial_change, 'bus', scatter_dimension=2, tiled=True)  219 us
    dot_general x11, matrix products, backward(): jnp.einsum('fjc,fhc->fjh', fetched_entries, operator_table, preferred_ele...  105 us
    dot_general x11, matrix products, forward(): jnp.einsum('hkj,hjf->hkf', state_now.astype(jnp.bfloat16), operator_table...  88.4 us
    all_gather x1, waiting for transfers between devices, shards(): piece_cols = lax.all_gather(network_row_block, 'bus', axis=1, tiled=True)  70.2 us
    unnamed x4, waiting for transfers between devices  67.6 us
    all_gather x1, blocking collectives, shards(): new_price = lax.all_gather(new_share, 'gen', axis=0, tiled=True)  19.2 us
    dynamic_update_slice x11, other arithmetic, smoothed_plan(): lax.scan(forward, opening, weights[1:])  14.5 us
  transfers between devices with their start and end apart: 3, of which 3 were waited for; matrix products, arithmetic and copies ran while one was open for 1% of the time, Pallas kernels for 0%

commit v1 on v0

--- a/solution.py
+++ b/solution.py
@@ -8,6 +8,13 @@
 NNZB = 16
 HIGHEST_PRECISION = lax.Precision.HIGHEST
 STEP_SIZE = 1.0
+
+
+def gather_over(array, axis, d):
+    peers = lax.axis_size(axis)
+    parts = jnp.stack([array for _ in range(peers)])
+    parts = lax.all_to_all(parts, axis, split_axis=0, concat_axis=0)
+    return jnp.concatenate(parts, axis=d)
 
 
 def successor_matrix(trans_rows, state_span):
@@ -92,7 +99,7 @@
     network_row_block = (injections - bus_demand).astype(jnp.bfloat16).reshape(row_total, bus_dev)
     line_blocks = ptdf_blocks.shape[0]
     wanted = ptdf_pattern.reshape(-1)
-    piece_cols = lax.all_gather(network_row_block, "bus", axis=1, tiled=True)
+    piece_cols = gather_over(network_row_block, "bus", 1)
     block_count = piece_cols.shape[1] // BLK
     block_ids = jnp.arange(block_count, dtype=jnp.int32)
     chooser = (wanted[:, None] == block_ids[None, :]).astype(jnp.bfloat16)

time: 692 us -> 672 us (0.971)
  waiting for transfers between devices: 357 us -> 319 us
  starting transfers between devices: 0.3 us -> 9.91 us
    all_gather x1 -> x0, waiting for transfers between devices: 70.2 us -> none  [shards(): piece_cols = lax.all_gather(network_row_block, 'bus', axis=1, tiled=True)]
    all_to_all x0 -> x1, waiting for transfers between devices: none -> 34.4 us  [gather_over(): parts = lax.all_to_all(parts, axis, split_axis=0, concat_axis=0)]
    all_to_all x0 -> x1, starting transfers between devices: none -> 9.65 us  [gather_over(): parts = lax.all_to_all(parts, axis, split_axis=0, concat_axis=0)]
    another operation x2 -> x5, local copies, waits for them, and re-layouts: 11.5 us -> 16.6 us
    unnamed x4 -> x3, waiting for transfers between devices: 67.6 us -> 67.7 us
where the time goes in v1:
time: 672 us; the launch traced here: 668 us
  waiting for transfers between devices  319 us (47%)
  matrix products  206 us (31%)
  local copies, waits for them, and re-layouts  63.1 us (9%)
  other arithmetic  35.4 us (5%)
  blocking collectives  19.6 us (3%)
  between operations  14.9 us (2%)
  starting transfers between devices  9.91 us (1%)
    reduce_scatter x1, waiting for transfers between devices, shards(): lax.psum_scatter(partial_change, 'bus', scatter_dimension=2, tiled=True)  217 us
    dot_general x11, matrix products, backward(): jnp.einsum('fjc,fhc->fjh', fetched_entries, operator_table, preferred_ele...  105 us
    dot_general x11, matrix products, forward(): jnp.einsum('hkj,hjf->hkf', state_now.astype(jnp.bfloat16), operator_table...  88.4 us
    unnamed x3, waiting for transfers between devices  67.7 us
    all_to_all x1, waiting for transfers between devices, gather_over(): parts = lax.all_to_all(parts, axis, split_axis=0, concat_axis=0)  34.4 us
    all_gather x1, blocking collectives, shards(): new_price = lax.all_gather(new_share, 'gen', axis=0, tiled=True)  19.6 us
    dynamic_update_slice x11, other arithmetic, smoothed_plan(): lax.scan(forward, opening, weights[1:])  14.5 us
    while x11, local copies, waits for them, and re-layouts  13.5 us
  transfers between devices with their start and end apart: 3, of which 3 were waited for; matrix products, arithmetic and copies ran while one was open for 1% of the time, Pallas kernels for 0%

profile of v1, /device:TPU:1, one launch (start us, length us, event | category | flops | bytes accessed | tf_op | source)
XLA Modules:
  0.0 668.1 jit_solution(3912871025889968397)
XLA Ops:
  8.8 2.0 convolution_bitcast_fusion.2
  10.8 3.3 exponential_multiply_fusion
  15.4 3.4 copy-done.1
  19.9 11.2 %slice.31 = f32[11,16,32,512]{3,2,1,0:T(8,128)} slice(f32[12,16,32,512]{3,2,1,0:T(8,128)} %copy-done.1), slice={[1:12], [0:16], [0:32], [0:512]} | slice | bytes 23068672 | tf_op jit(solution)/shard_map/slice | solution.py:48
  31.1 5.7 broadcast.50.clone
  36.8 103.0 %while.32 = (s32[]{:T(128)}, bf16[16,32,512]{2,1,0:T(8,128)(2,1)}, f32[11,16,32,512]{3,2,1,0:T(8,128)}, f32[11,16,32,1]{2,1,3,0:T(8,128)S(1)}, f32[11,16,32,512]...) while((s32[]{:T(128)}, bf16[16,32,512]{2,1,0:T(8,128)(2,1)}, ...), condition=%wide.region_3.4_spmd.clone, body=%wide.region_1.3_spmd.clone.sunk | while | flops 319815168 | bytes 5361777 | solution.py:48
  36.8 8.0 %fusion.75 = (f32[16,32]{1,0:T(8,128)S(1)}, f32[16,32,512]{2,1,0:T(8,128)S(1)}) fusion(f32[11,16,32,512]{3,2,1,0:T(8,128)} %get-tuple-element.389, s32[]{:T(128)S(6)} %copy.77, s32[16,512]{1,0:T(8,128)S(1)} %get-tuple-element.392, s32[16,512]{1,0:T(8,128)S(1)} %get-tuple-element.391, s32[16,512]{1,0:T(8,128)S(1)} %get-tuple-element.390, ...), kind=kOutput, calls=%fused_computation.83.clone.1 | convolution fusion | flops 319290880 | bytes 2721796 | tf_op jit(solution)/shard_map/while/body/eval_jaxpr/hkj,hjf->hkf/dot_general | solution.py:37
  44.8 1.3 bitcast_dynamic-update-slice_fusion.6
  46.1 8.0 %fusion.75 = (f32[16,32]{1,0:T(8,128)S(1)}, f32[16,32,512]{2,1,0:T(8,128)S(1)}) fusion(f32[11,16,32,512]{3,2,1,0:T(8,128)} %get-tuple-element.389, s32[]{:T(128)S(6)} %copy.77, s32[16,512]{1,0:T(8,128)S(1)} %get-tuple-element.392, s32[16,512]{1,0:T(8,128)S(1)} %get-tuple-element.391, s32[16,512]{1,0:T(8,128)S(1)} %get-tuple-element.390, ...), kind=kOutput, calls=%fused_computation.83.clone.1 | convolution fusion | flops 319290880 | bytes 2721796 | tf_op jit(solution)/shard_map/while/body/eval_jaxpr/hkj,hjf->hkf/dot_general | solution.py:37
  54.2 1.3 bitcast_dynamic-update-slice_fusion.6
  55.5 8.0 %fusion.75 = (f32[16,32]{1,0:T(8,128)S(1)}, f32[16,32,512]{2,1,0:T(8,128)S(1)}) fusion(f32[11,16,32,512]{3,2,1,0:T(8,128)} %get-tuple-element.389, s32[]{:T(128)S(6)} %copy.77, s32[16,512]{1,0:T(8,128)S(1)} %get-tuple-element.392, s32[16,512]{1,0:T(8,128)S(1)} %get-tuple-element.391, s32[16,512]{1,0:T(8,128)S(1)} %get-tuple-element.390, ...), kind=kOutput, calls=%fused_computation.83.clone.1 | convolution fusion | flops 319290880 | bytes 2721796 | tf_op jit(solution)/shard_map/while/body/eval_jaxpr/hkj,hjf->hkf/dot_general | solution.py:37
  63.6 1.3 bitcast_dynamic-update-slice_fusion.6
  64.9 8.0 %fusion.75 = (f32[16,32]{1,0:T(8,128)S(1)}, f32[16,32,512]{2,1,0:T(8,128)S(1)}) fusion(f32[11,16,32,512]{3,2,1,0:T(8,128)} %get-tuple-element.389, s32[]{:T(128)S(6)} %copy.77, s32[16,512]{1,0:T(8,128)S(1)} %get-tuple-element.392, s32[16,512]{1,0:T(8,128)S(1)} %get-tuple-element.391, s32[16,512]{1,0:T(8,128)S(1)} %get-tuple-element.390, ...), kind=kOutput, calls=%fused_computation.83.clone.1 | convolution fusion | flops 319290880 | bytes 2721796 | tf_op jit(solution)/shard_map/while/body/eval_jaxpr/hkj,hjf->hkf/dot_general | solution.py:37
  72.9 1.3 bitcast_dynamic-update-slice_fusion.6
  74.2 8.0 %fusion.75 = (f32[16,32]{1,0:T(8,128)S(1)}, f32[16,32,512]{2,1,0:T(8,128)S(1)}) fusion(f32[11,16,32,512]{3,2,1,0:T(8,128)} %get-tuple-element.389, s32[]{:T(128)S(6)} %copy.77, s32[16,512]{1,0:T(8,128)S(1)} %get-tuple-element.392, s32[16,512]{1,0:T(8,128)S(1)} %get-tuple-element.391, s32[16,512]{1,0:T(8,128)S(1)} %get-tuple-element.390, ...), kind=kOutput, calls=%fused_computation.83.clone.1 | convolution fusion | flops 319290880 | bytes 2721796 | tf_op jit(solution)/shard_map/while/body/eval_jaxpr/hkj,hjf->hkf/dot_general | solution.py:37
  82.3 1.3 bitcast_dynamic-update-slice_fusion.6
  83.6 8.0 %fusion.75 = (f32[16,32]{1,0:T(8,128)S(1)}, f32[16,32,512]{2,1,0:T(8,128)S(1)}) fusion(f32[11,16,32,512]{3,2,1,0:T(8,128)} %get-tuple-element.389, s32[]{:T(128)S(6)} %copy.77, s32[16,512]{1,0:T(8,128)S(1)} %get-tuple-element.392, s32[16,512]{1,0:T(8,128)S(1)} %get-tuple-element.391, s32[16,512]{1,0:T(8,128)S(1)} %get-tuple-element.390, ...), kind=kOutput, calls=%fused_computation.83.clone.1 | convolution fusion | flops 319290880 | bytes 2721796 | tf_op jit(solution)/shard_map/while/body/eval_jaxpr/hkj,hjf->hkf/dot_general | solution.py:37
  91.6 1.3 bitcast_dynamic-update-slice_fusion.6
  93.0 8.0 %fusion.75 = (f32[16,32]{1,0:T(8,128)S(1)}, f32[16,32,512]{2,1,0:T(8,128)S(1)}) fusion(f32[11,16,32,512]{3,2,1,0:T(8,128)} %get-tuple-element.389, s32[]{:T(128)S(6)} %copy.77, s32[16,512]{1,0:T(8,128)S(1)} %get-tuple-element.392, s32[16,512]{1,0:T(8,128)S(1)} %get-tuple-element.391, s32[16,512]{1,0:T(8,128)S(1)} %get-tuple-element.390, ...), kind=kOutput, calls=%fused_computation.83.clone.1 | convolution fusion | flops 319290880 | bytes 2721796 | tf_op jit(solution)/shard_map/while/body/eval_jaxpr/hkj,hjf->hkf/dot_general | solution.py:37
  101.0 1.3 bitcast_dynamic-update-slice_fusion.6
  102.3 8.0 %fusion.75 = (f32[16,32]{1,0:T(8,128)S(1)}, f32[16,32,512]{2,1,0:T(8,128)S(1)}) fusion(f32[11,16,32,512]{3,2,1,0:T(8,128)} %get-tuple-element.389, s32[]{:T(128)S(6)} %copy.77, s32[16,512]{1,0:T(8,128)S(1)} %get-tuple-element.392, s32[16,512]{1,0:T(8,128)S(1)} %get-tuple-element.391, s32[16,512]{1,0:T(8,128)S(1)} %get-tuple-element.390, ...), kind=kOutput, calls=%fused_computation.83.clone.1 | convolution fusion | flops 319290880 | bytes 2721796 | tf_op jit(solution)/shard_map/while/body/eval_jaxpr/hkj,hjf->hkf/dot_general | solution.py:37
  110.4 1.3 bitcast_dynamic-update-slice_fusion.6
  111.7 8.0 %fusion.75 = (f32[16,32]{1,0:T(8,128)S(1)}, f32[16,32,512]{2,1,0:T(8,128)S(1)}) fusion(f32[11,16,32,512]{3,2,1,0:T(8,128)} %get-tuple-element.389, s32[]{:T(128)S(6)} %copy.77, s32[16,512]{1,0:T(8,128)S(1)} %get-tuple-element.392, s32[16,512]{1,0:T(8,128)S(1)} %get-tuple-element.391, s32[16,512]{1,0:T(8,128)S(1)} %get-tuple-element.390, ...), kind=kOutput, calls=%fused_computation.83.clone.1 | convolution fusion | flops 319290880 | bytes 2721796 | tf_op jit(solution)/shard_map/while/body/eval_jaxpr/hkj,hjf->hkf/dot_general | solution.py:37
  119.7 1.3 bitcast_dynamic-update-slice_fusion.6
  121.1 8.0 %fusion.75 = (f32[16,32]{1,0:T(8,128)S(1)}, f32[16,32,512]{2,1,0:T(8,128)S(1)}) fusion(f32[11,16,32,512]{3,2,1,0:T(8,128)} %get-tuple-element.389, s32[]{:T(128)S(6)} %copy.77, s32[16,512]{1,0:T(8,128)S(1)} %get-tuple-element.392, s32[16,512]{1,0:T(8,128)S(1)} %get-tuple-element.391, s32[16,512]{1,0:T(8,128)S(1)} %get-tuple-element.390, ...), kind=kOutput, calls=%fused_computation.83.clone.1 | convolution fusion | flops 319290880 | bytes 2721796 | tf_op jit(solution)/shard_map/while/body/eval_jaxpr/hkj,hjf->hkf/dot_general | solution.py:37
  129.1 1.3 bitcast_dynamic-update-slice_fusion.6
  130.4 8.0 %fusion.75 = (f32[16,32]{1,0:T(8,128)S(1)}, f32[16,32,512]{2,1,0:T(8,128)S(1)}) fusion(f32[11,16,32,512]{3,2,1,0:T(8,128)} %get-tuple-element.389, s32[]{:T(128)S(6)} %copy.77, s32[16,512]{1,0:T(8,128)S(1)} %get-tuple-element.392, s32[16,512]{1,0:T(8,128)S(1)} %get-tuple-element.391, s32[16,512]{1,0:T(8,128)S(1)} %get-tuple-element.390, ...), kind=kOutput, calls=%fused_computation.83.clone.1 | convolution fusion | flops 319290880 | bytes 2721796 | tf_op jit(solution)/shard_map/while/body/eval_jaxpr/hkj,hjf->hkf/dot_general | solution.py:37
  138.5 1.3 bitcast_dynamic-update-slice_fusion.6
  140.9 5.8 broadcast.50
  146.7 118.4 %while.33 = (s32[]{:T(128)}, f32[16,32,512]{2,1,0:T(8,128)}, f32[11,16,32,512]{3,2,1,0:T(8,128)}, f32[11,16,32,512]{3,2,1,0:T(8,128)}, f32[11,16,32,1]{2,1,3,0:T...) while((s32[]{:T(128)}, f32[16,32,512]{2,1,0:T(8,128)}, ...), condition=%wide.region_5.6_spmd.clone, body=%wide.region_4.5_spmd.clone.sunk | while | flops 319553536 | bytes 6397045 | solution.py:60
  146.7 1.2 copy.96
  148.0 9.5 %bitcast_dynamic-update-slice_fusion.8 = (f32[11,16,32,512]{3,2,1,0:T(8,128)}, f32[16,32,512]{2,1,0:T(8,128)}) fusion(f32[11,16,32,512]{3,2,1,0:T(8,128)} %get-tuple-element.406, s32[]{:T(128)S(6)} %sub.131, s32[16,512]{1,0:T(8,128)S(1)} %get-tuple-element.421, s32[16,512]{1,0:T(8,128)S(1)} %get-tuple-element.420, ...), kind=kOutput, calls=%fused_computation.31.clone.1 | convolution fusion | flops 319553536 | bytes 4295680 | tf_op jit(solution)/shard_map/while/body/eval_jaxpr/fjc,fhc->fjh/dot_general | solution.py:54
  157.5 1.2 copy.96
  158.7 9.5 %bitcast_dynamic-update-slice_fusion.8 = (f32[11,16,32,512]{3,2,1,0:T(8,128)}, f32[16,32,512]{2,1,0:T(8,128)}) fusion(f32[11,16,32,512]{3,2,1,0:T(8,128)} %get-tuple-element.406, s32[]{:T(128)S(6)} %sub.131, s32[16,512]{1,0:T(8,128)S(1)} %get-tuple-element.421, s32[16,512]{1,0:T(8,128)S(1)} %get-tuple-element.420, ...), kind=kOutput, calls=%fused_computation.31.clone.1 | convolution fusion | flops 319553536 | bytes 4295680 | tf_op jit(solution)/shard_map/while/body/eval_jaxpr/fjc,fhc->fjh/dot_general | solution.py:54
  168.3 1.2 copy.96
  169.5 9.5 %bitcast_dynamic-update-slice_fusion.8 = (f32[11,16,32,512]{3,2,1,0:T(8,128)}, f32[16,32,512]{2,1,0:T(8,128)}) fusion(f32[11,16,32,512]{3,2,1,0:T(8,128)} %get-tuple-element.406, s32[]{:T(128)S(6)} %sub.131, s32[16,512]{1,0:T(8,128)S(1)} %get-tuple-element.421, s32[16,512]{1,0:T(8,128)S(1)} %get-tuple-element.420, ...), kind=kOutput, calls=%fused_computation.31.clone.1 | convolution fusion | flops 319553536 | bytes 4295680 | tf_op jit(solution)/shard_map/while/body/eval_jaxpr/fjc,fhc->fjh/dot_general | solution.py:54
  179.1 1.2 copy.96
  180.3 9.5 %bitcast_dynamic-update-slice_fusion.8 = (f32[11,16,32,512]{3,2,1,0:T(8,128)}, f32[16,32,512]{2,1,0:T(8,128)}) fusion(f32[11,16,32,512]{3,2,1,0:T(8,128)} %get-tuple-element.406, s32[]{:T(128)S(6)} %sub.131, s32[16,512]{1,0:T(8,128)S(1)} %get-tuple-element.421, s32[16,512]{1,0:T(8,128)S(1)} %get-tuple-element.420, ...), kind=kOutput, calls=%fused_computation.31.clone.1 | convolution fusion | flops 319553536 | bytes 4295680 | tf_op jit(solution)/shard_map/while/body/eval_jaxpr/fjc,fhc->fjh/dot_general | solution.py:54
  189.8 1.2 copy.96
  191.0 9.6 %bitcast_dynamic-update-slice_fusion.8 = (f32[11,16,32,512]{3,2,1,0:T(8,128)}, f32[16,32,512]{2,1,0:T(8,128)}) fusion(f32[11,16,32,512]{3,2,1,0:T(8,128)} %get-tuple-element.406, s32[]{:T(128)S(6)} %sub.131, s32[16,512]{1,0:T(8,128)S(1)} %get-tuple-element.421, s32[16,512]{1,0:T(8,128)S(1)} %get-tuple-element.420, ...), kind=kOutput, calls=%fused_computation.31.clone.1 | convolution fusion | flops 319553536 | bytes 4295680 | tf_op jit(solution)/shard_map/while/body/eval_jaxpr/fjc,fhc->fjh/dot_general | solution.py:54
  201.8 9.5 %bitcast_dynamic-update-slice_fusion.8 = (f32[11,16,32,512]{3,2,1,0:T(8,128)}, f32[16,32,512]{2,1,0:T(8,128)}) fusion(f32[11,16,32,512]{3,2,1,0:T(8,128)} %get-tuple-element.406, s32[]{:T(128)S(6)} %sub.131, s32[16,512]{1,0:T(8,128)S(1)} %get-tuple-element.421, s32[16,512]{1,0:T(8,128)S(1)} %get-tuple-element.420, ...), kind=kOutput, calls=%fused_computation.31.clone.1 | convolution fusion | flops 319553536 | bytes 4295680 | tf_op jit(solution)/shard_map/while/body/eval_jaxpr/fjc,fhc->fjh/dot_general | solution.py:54
  212.6 9.5 %bitcast_dynamic-update-slice_fusion.8 = (f32[11,16,32,512]{3,2,1,0:T(8,128)}, f32[16,32,512]{2,1,0:T(8,128)}) fusion(f32[11,16,32,512]{3,2,1,0:T(8,128)} %get-tuple-element.406, s32[]{:T(128)S(6)} %sub.131, s32[16,512]{1,0:T(8,128)S(1)} %get-tuple-element.421, s32[16,512]{1,0:T(8,128)S(1)} %get-tuple-element.420, ...), kind=kOutput, calls=%fused_computation.31.clone.1 | convolution fusion | flops 319553536 | bytes 4295680 | tf_op jit(solution)/shard_map/while/body/eval_jaxpr/fjc,fhc->fjh/dot_general | solution.py:54
  223.4 9.5 %bitcast_dynamic-update-slice_fusion.8 = (f32[11,16,32,512]{3,2,1,0:T(8,128)}, f32[16,32,512]{2,1,0:T(8,128)}) fusion(f32[11,16,32,512]{3,2,1,0:T(8,128)} %get-tuple-element.406, s32[]{:T(128)S(6)} %sub.131, s32[16,512]{1,0:T(8,128)S(1)} %get-tuple-element.421, s32[16,512]{1,0:T(8,128)S(1)} %get-tuple-element.420, ...), kind=kOutput, calls=%fused_computation.31.clone.1 | convolution fusion | flops 319553536 | bytes 4295680 | tf_op jit(solution)/shard_map/while/body/eval_jaxpr/fjc,fhc->fjh/dot_general | solution.py:54
  234.1 9.5 %bitcast_dynamic-update-slice_fusion.8 = (f32[11,16,32,512]{3,2,1,0:T(8,128)}, f32[16,32,512]{2,1,0:T(8,128)}) fusion(f32[11,16,32,512]{3,2,1,0:T(8,128)} %get-tuple-element.406, s32[]{:T(128)S(6)} %sub.131, s32[16,512]{1,0:T(8,128)S(1)} %get-tuple-element.421, s32[16,512]{1,0:T(8,128)S(1)} %get-tuple-element.420, ...), kind=kOutput, calls=%fused_computation.31.clone.1 | convolution fusion | flops 319553536 | bytes 4295680 | tf_op jit(solution)/shard_map/while/body/eval_jaxpr/fjc,fhc->fjh/dot_general | solution.py:54
  244.9 9.5 %bitcast_dynamic-update-slice_fusion.8 = (f32[11,16,32,512]{3,2,1,0:T(8,128)}, f32[16,32,512]{2,1,0:T(8,128)}) fusion(f32[11,16,32,512]{3,2,1,0:T(8,128)} %get-tuple-element.406, s32[]{:T(128)S(6)} %sub.131, s32[16,512]{1,0:T(8,128)S(1)} %get-tuple-element.421, s32[16,512]{1,0:T(8,128)S(1)} %get-tuple-element.420, ...), kind=kOutput, calls=%fused_computation.31.clone.1 | convolution fusion | flops 319553536 | bytes 4295680 | tf_op jit(solution)/shard_map/while/body/eval_jaxpr/fjc,fhc->fjh/dot_general | solution.py:54
  255.6 9.5 %bitcast_dynamic-update-slice_fusion.8 = (f32[11,16,32,512]{3,2,1,0:T(8,128)}, f32[16,32,512]{2,1,0:T(8,128)}) fusion(f32[11,16,32,512]{3,2,1,0:T(8,128)} %get-tuple-element.406, s32[]{:T(128)S(6)} %sub.131, s32[16,512]{1,0:T(8,128)S(1)} %get-tuple-element.421, s32[16,512]{1,0:T(8,128)S(1)} %get-tuple-element.420, ...), kind=kOutput, calls=%fused_computation.31.clone.1 | convolution fusion | flops 319553536 | bytes 4295680 | tf_op jit(solution)/shard_map/while/body/eval_jaxpr/fjc,fhc->fjh/dot_general | solution.py:54
  265.2 8.9 %fusion.37 = (f32[12,16,32]{2,1,0:T(8,128)S(1)}, f32[12,16,32]{2,1,0:T(8,128)S(1)}) fusion(f32[11,16,32,512]{3,2,1,0:T(8,128)} %get-tuple-element.159, f32[11,16,32,512]{3,2,1,0:T(8,128)} %get-tuple-element.157, f32[1,16,32,512]{3,2,1,0:T(8,128)} %slice_divide_fusion, f32[16,512]{1,0:T(8,128)S(1)} %copy-done.4), kind=kLoop, calls=%fused_computation.41 | loop fusion | flops 15716352 | bytes 24199168 | tf_op jit(solution)/shard_map/reduce_sum | solution.py:63
  274.0 1.4 convolution_bitcast_fusion.1
  276.7 67.6 %all-reduce.4.cloned.1.call-done = f32[32,12,512]{2,0,1:T(8,128)} async-done(((f32[32,12,512]{2,0,1:T(8,128)}), f32[32,12,512]{2,0,1:T(8,128)}) %all-reduce.4.cloned.1.call-update) | async-done | bytes 786448
  345.4 1.3 stack.8
  346.8 9.7 %all-to-all-start = ((bf16[32,48,512]{2,1,0:T(8,128)(2,1)}), bf16[32,48,512]{2,1,0:T(8,128)(2,1)}, u32[]{:S(2)}, u32[]{:S(2)}) async-start(bf16[32,48,512]{2,1,0:T(8,128)(2,1)} %stack.8), calls=%async_computation | async-start | bytes 3145728 | tf_op jit(solution)/shard_map/all_to_all | solution.py:16
  358.2 34.4 %all-to-all-done = bf16[32,48,512]{2,1,0:T(8,128)(2,1)} async-done(((bf16[32,48,512]{2,1,0:T(8,128)(2,1)}), bf16[32,48,512]{2,1,0:T(8,128)(2,1)}, u32[]{:S(2)}, u32[]{:S(2)}) %all-to-all-start) | async-done | bytes 1572896 | tf_op jit(solution)/shard_map/all_to_all | solution.py:16
  392.6 3.4 copy.29
  396.0 3.8 reshape_reshape.3
  399.7 1.9 convolution_convert_fusion
  404.2 1.9 add_maximum_fusion.1
  406.1 1.6 squeeze.27
  407.7 1.6 squeeze.26
  409.3 2.3 convolution_bitcast_fusion
  411.6 4.0 fusion.40
  415.6 3.6 reshape.82
  422.1 217.3 %reduce-scatter.3.cloned.1.call-done = f32[4,12,512]{2,1,0:T(8,128)} async-done(((f32[4,12,16384]{2,1,0:T(8,128)}), f32[4,12,512]{2,1,0:T(8,128)}) %reduce-scatter.3.cloned.1.call-update) | async-done | bytes 98320 | tf_op jit(solution)/shard_map/reduce_scatter | solution.py:127
  640.3 19.6 %all_gather.3 = f32[32,12,512]{2,1,0:T(8,128)S(1)} all-gather(f32[4,12,512]{2,1,0:T(8,128)S(1)} %copy_subtract_fusion), channel_id=1, replica_groups=mesh['gen'=8,'bus'=32] {'gen'}, dimensions={0}, use_global_device_ids=true | all-gather | bytes 884736 | tf_op jit(solution)/shard_map/all_gather | solution.py:130
  659.9 1.3 copy.40
  (70 shorter events, 22.2 us)
Async XLA Ops:
  7.2 394.5 %copy-start = (bf16[6,16,128,128]{3,2,1,0:T(8,128)(2,1)S(1)}, bf16[6,16,128,128]{3,2,1,0:T(8,128)(2,1)}, u32[]{:S(2)}) copy-start(bf16[6,16,128,128]{3,2,1,0:T(8,128)(2,1)} %param.19) | copy-start | bytes 9437188
  7.2 337.2 %all-reduce.4.cloned.1.call-start = ((), (), s32[]{:S(2)}) async-start(), calls=%async_computation.3 | async-start | bytes 1572864
  14.2 4.7 copy-start.1
  19.9 11.2 %copy-start.5 = (s32[16,3,512]{2,0,1:T(8,128)S(1)}, s32[16,3,512]{2,0,1:T(8,128)}, u32[]{:S(2)}) copy-start(s32[16,3,512]{2,0,1:T(8,128)} %param.23) | copy-start | bytes 294916
  146.7 118.4 %copy-start.4 = (f32[16,512]{1,0:T(8,128)S(1)}, f32[16,512]{1,0:T(8,128)}, u32[]{:S(2)}) copy-start(f32[16,512]{1,0:T(8,128)} %param.24) | copy-start | bytes 98308
  265.2 10.3 %copy-start.8 = (u32[256]{0:T(256)S(1)}, u32[256]{0:T(256)}, u32[]{:S(2)}) copy-start(u32[256]{0:T(256)} %constant.88) | copy-start | bytes 3076
  265.2 92.3 %copy-start.3 = (f32[2,4,12,768]{3,1,2,0:T(4,128)S(1)}, f32[2,4,12,768]{3,1,2,0:T(4,128)}, u32[]{:S(2)}) copy-start(f32[2,4,12,768]{3,1,2,0:T(4,128)} %param.17) | copy-start | bytes 884740
  345.4 58.8 %copy-start.6 = (f32[768]{0:T(1024)S(1)}, f32[768]{0:T(1024)}, u32[]{:S(2)}) copy-start(f32[768]{0:T(1024)} %param.18) | copy-start | bytes 9220
  346.8 45.8 %all-to-all-start = ((bf16[32,48,512]{2,1,0:T(8,128)(2,1)}), bf16[32,48,512]{2,1,0:T(8,128)(2,1)}, u32[]{:S(2)}, u32[]{:S(2)}) async-start(bf16[32,48,512]{2,1,0:T(8,128)(2,1)} %stack.8), calls=%async_computation | async-start | bytes 3145728 | tf_op jit(solution)/shard_map/all_to_all | solution.py:16
  356.4 283.0 %reduce-scatter.3.cloned.1.call-start = ((), (), s32[]{:S(2)}) async-start(), calls=%async_computation.2 | async-start | bytes 4325376 | tf_op jit(solution)/shard_map/reduce_scatter | solution.py:127
  396.0 15.6 %copy-start.7 = (s32[6,16]{1,0:T(8,128)S(1)}, s32[6,16]{1,0:T(8,128)}, u32[]{:S(2)}) copy-start(s32[6,16]{1,0:T(8,128)} %param.20) | copy-start | bytes 1156
  409.3 10.9 %copy-start.2 = (f32[1,4,12,768]{3,2,1,0:T(8,128)S(1)}, f32[1,4,12,768]{3,2,1,0:T(8,128)}, u32[]{:S(2)}) copy-start(f32[1,4,12,768]{3,2,1,0:T(8,128)} %get-tuple-element.248) | copy-start | bytes 442372
Sparse Core Ops, SparseCore 0:
  275.6 68.7 all-reduce.3
  419.4 219.9 reduce-scatter.2
